TPU v7x, 256 devices: a whole 4x4x8 slice. The times are simulated.
256 devices in a mesh: row: 8 (over x, z_lo), col: 32 (over y, z_hi, core).
Axes of the slice: x: 4, y: 4, z: 8 (z_hi: 4, z_lo: 2; z = z_hi * 2 + z_lo), core: 2. Of those that a mesh axis runs over, the one named last changes fastest.
Arguments:
- hamiltonian: float32 [4096, 4096], P('row', 'col'), as said below
- h_mask: int32 [32, 32], P('row', 'col'), may hold values from 0 to 1, as said below
- factor: float32 [4096, 4096], P('row', 'col'), may hold values from -0.125 to 0.125
- z_mask: int32 [32, 32], P('row', 'col'), may hold values 0 or 1
- k_mask: int32 [32, 32], P('row', 'col'), may hold values 0 or 1
- block_sizes: int32 [32], replicated, may hold values from 64 to 128, as said below
Outputs:
- transformed: float32 [4096, 4096], P('row', 'col')
Inputs may be any that keep to these rules, and one draw needn't show every extreme that they name: hamiltonian is symmetric. `h_mask`: symmetric, with every diagonal block occupied. `block_sizes`: some block uses all 128 orbitals.
All inputs are finite; a program needn't handle non-finite values. No bound on the sum of `z_mask` or of `k_mask` on one device may be relied on, other than what follows from the above.
Results may differ from a plain program's by a relative error of at most 0.000098.
Values sent between devices are 32-bit elements; how exact they have to be, the bound alone decides.
A program may use at most 64 MiB of HBM per device.

v0:
```python
import jax
import jax.numpy as jnp
from jax import lax
from jax.sharding import PartitionSpec as P

BLOCK = 128


def expand(blocks):
    grown = jnp.repeat(blocks.astype(jnp.float32), BLOCK, axis=0)
    return jnp.repeat(grown, BLOCK, axis=1)


def validity(block_sizes, first, count):
    sizes = lax.dynamic_slice_in_dim(block_sizes, first, count, 0)
    within = jnp.arange(BLOCK, dtype=jnp.int32)
    return (within[None, :] < sizes[:, None]).astype(jnp.float32).reshape(-1)


def local(hamiltonian, h_mask, factor, z_mask, k_mask, block_sizes):
    rows_here, cols_here = hamiltonian.shape
    row_blocks = rows_here // BLOCK
    col_blocks = cols_here // BLOCK
    row_place = lax.axis_index("row")
    row_first = row_place * row_blocks
    col_first = lax.axis_index("col") * col_blocks
    row_valid = validity(block_sizes, row_first, row_blocks)
    col_valid = validity(block_sizes, col_first, col_blocks)
    outer = row_valid[:, None] * col_valid[None, :]
    global_rows = row_first * BLOCK + jnp.arange(rows_here, dtype=jnp.int32)
    global_cols = col_first * BLOCK + jnp.arange(cols_here, dtype=jnp.int32)
    upper = (global_rows[:, None] <= global_cols[None, :]).astype(jnp.float32)
    hmat = hamiltonian * expand(h_mask) * outer
    zmat = factor * expand(z_mask) * outer * upper
    highest = lax.Precision.HIGHEST
    zcolumn = lax.all_gather(zmat, "row", axis=0, tiled=True)
    hz_tile = jnp.dot(
        lax.all_gather(hmat, "col", axis=1, tiled=True),
        zcolumn,
        precision=highest,
        preferred_element_type=jnp.float32,
    )
    terms = jnp.dot(
        lax.all_gather(zmat, "col", axis=1, tiled=True).T,
        hz_tile,
        precision=highest,
        preferred_element_type=jnp.float32,
    )
    result = lax.psum_scatter(terms, "row", scatter_dimension=0, tiled=True)
    return result * expand(k_mask)


def solution(mesh):
    placed = (
        P("row", "col"),
        P("row", "col"),
        P("row", "col"),
        P("row", "col"),
        P("row", "col"),
        P(),
    )
    return jax.shard_map(
        local, mesh=mesh, in_specs=placed, out_specs=P("row", "col"), check_vma=False
    )
```

profile of v0, /device:TPU:1, one launch (start us, length us, event | category | flops | bytes accessed | tf_op | source)
XLA Modules:
  0.0 323.2 jit_solution(6343206805627346707)
XLA Ops:
  6.5 0.0 all-gather.8.cloned.1.call-start
  6.5 0.7 dynamic_slice.6
  7.3 0.1 convert_bitcast_fusion
  7.3 1.2 dynamic_slice.7
  8.6 0.6 compare_convert_fusion
  9.3 0.7 convert_bitcast_fusion.2
  9.9 0.7 convert_bitcast_fusion.3
  10.6 0.1 broadcast_bitcast_fusion.1
  10.7 2.1 multiply_multiply_fusion
  12.8 0.0 all-gather.8.cloned.1.call-update
  12.8 0.0 all-gather.6.cloned.1.call-start
  12.9 0.7 all-gather.6.cloned.1.call-update
  13.6 0.0 all-gather.4.cloned.1.call-start
  13.6 0.7 all-gather.4.cloned.1.call-update
  14.3 0.0 reduce-scatter.2.cloned.1.call-start
  14.3 56.9 %all-gather.8.cloned.1.call-done = f32[4096,128]{1,0:T(8,128)} async-done(((f32[512,128]{1,0:T(8,128)}), f32[4096,128]{1,0:T(8,128)}) %all-gather.8.cloned.1.call-update) | async-done | bytes 2097168 | tf_op jit(solution)/shard_map/all_gather | solution.py:36
  71.2 88.0 %all-gather.6.cloned.1.call-done = f32[512,4096]{1,0:T(8,128)} async-done(((f32[512,128]{1,0:T(8,128)}), f32[512,4096]{1,0:T(8,128)}) %all-gather.6.cloned.1.call-update) | async-done | bytes 8388624 | tf_op jit(solution)/shard_map/all_gather | solution.py:38
  159.3 9.3 %fusion.1 = f32[512,128]{1,0:T(8,128)S(1)} fusion(f32[512,4096]{1,0:T(8,128)} %all-gather.6.cloned.1.call-done, f32[4096,128]{1,0:T(8,128)} %all-gather.8.cloned.1.call-done), kind=kOutput, calls=%fused_computation.15 | convolution fusion | flops 3221225472 | bytes 10747904 | tf_op jit(solution)/shard_map/dot_general | solution.py:37
  168.6 0.0 copy-start
  168.6 76.9 %all-gather.4.cloned.1.call-done = f32[512,4096]{1,0:T(8,128)} async-done(((f32[512,128]{1,0:T(8,128)}), f32[512,4096]{1,0:T(8,128)}) %all-gather.4.cloned.1.call-update) | async-done | bytes 8388624 | tf_op jit(solution)/shard_map/all_gather | solution.py:44
  245.6 16.5 %fusion.2 = f32[4096,128]{1,0:T(8,128)} fusion(f32[512,4096]{1,0:T(8,128)} %all-gather.4.cloned.1.call-done, f32[512,128]{1,0:T(8,128)S(1)} %fusion.1), kind=kOutput, calls=%fused_computation.16 | convolution fusion | flops 3221225472 | bytes 10747904 | tf_op jit(solution)/shard_map/dot_general | solution.py:43
  262.1 0.0 reduce-scatter.2.cloned.1.call-update
  262.1 0.0 copy-done
  262.1 0.1 broadcast_bitcast_fusion
  262.2 52.7 %reduce-scatter.2.cloned.1.call-done = f32[512,128]{1,0:T(8,128)} async-done(((f32[4096,128]{1,0:T(8,128)}), f32[512,128]{1,0:T(8,128)}) %reduce-scatter.2.cloned.1.call-update) | async-done | bytes 262160 | tf_op jit(solution)/shard_map/reduce_scatter | solution.py:49
  314.9 1.8 broadcast_multiply_fusion
  (3 shorter events, 0.0 us)
Async XLA Ops:
  6.5 64.7 %all-gather.8.cloned.1.call-start = ((), (), s32[]{:S(2)}) async-start(), calls=%async_computation.3 | async-start | bytes 2359296 | tf_op jit(solution)/shard_map/all_gather | solution.py:36
  12.8 146.4 %all-gather.6.cloned.1.call-start = ((), (), s32[]{:S(2)}) async-start(), calls=%async_computation.2 | async-start | bytes 8650752 | tf_op jit(solution)/shard_map/all_gather | solution.py:38
  13.6 232.0 %all-gather.4.cloned.1.call-start = ((), (), s32[]{:S(2)}) async-start(), calls=%async_computation.1 | async-start | bytes 8650752 | tf_op jit(solution)/shard_map/all_gather | solution.py:44
  14.3 300.6 %reduce-scatter.2.cloned.1.call-start = ((), (), s32[]{:S(2)}) async-start(), calls=%async_computation.4 | async-start | bytes 2359296 | tf_op jit(solution)/shard_map/reduce_scatter | solution.py:49
  168.6 93.5 %copy-start = (s32[4,1]{0,1:T(1,128)S(1)}, s32[4,1]{0,1:T(1,128)}, u32[]{:S(2)}) copy-start(s32[4,1]{0,1:T(1,128)} %param.10) | copy-start | bytes 52
Sparse Core Ops, SparseCore 0:
  12.9 58.2 all-gather.7
  73.7 85.4 all-gather.5
  161.7 83.7 all-gather.3
  262.2 52.6 reduce-scatter.1
where the time goes:
time: 323 us
  waiting for transfers between devices  276 us (85%)
  matrix products  25.9 us (8%)
  between operations  13.2 us (4%)
  other arithmetic  5.97 us (2%)
    all_gather x1, waiting for transfers between devices, local(): lax.all_gather(hmat, 'col', axis=1, tiled=True)  88 us
    all_gather x1, waiting for transfers between devices, local(): lax.all_gather(zmat, 'col', axis=1, tiled=True)  76.9 us
    all_gather x1, waiting for transfers between devices, local(): zcolumn = lax.all_gather(zmat, 'row', axis=0, tiled=True)  56.9 us
    reduce_scatter x1, waiting for transfers between devices, local(): result = lax.psum_scatter(terms, 'row', scatter_dimension=0, tiled=True)  52.7 us
    dot_general x1, matrix products, local(): jnp.dot(lax.all_gather(zmat, 'col', axis=1, tiled=True).T, hz_tile, preci...  16.5 us
    dot_general x1, matrix products, local(): jnp.dot(lax.all_gather(hmat, 'col', axis=1, tiled=True), zcolumn, precisi...  9.35 us
  transfers between devices with their start and end apart: 4, of which 4 were waited for; matrix products, arithmetic and copies ran while one was open for 3% of the time, Pallas kernels for 0%

commit v1 on v0

--- a/solution.py
+++ b/solution.py
@@ -1,9 +1,23 @@
+import functools
 import jax
 import jax.numpy as jnp
 from jax import lax
 from jax.sharding import PartitionSpec as P
 
 BLOCK = 128
+
+
+def reach_pipes(m, across):
+    outcome_arr = jnp.concatenate(
+        jax.lax.all_to_all(
+            jnp.stack(tuple((m for _ in range(jax.lax.axis_size(across)))), axis=0), across, 0, 0
+        ),
+        axis=1,
+    )
+    return outcome_arr
+
+
+change_tables = functools.partial(reach_pipes, across="col")
 
 
 def expand(blocks):
@@ -35,10 +49,7 @@
     highest = lax.Precision.HIGHEST
     zcolumn = lax.all_gather(zmat, "row", axis=0, tiled=True)
     hz_tile = jnp.dot(
-        lax.all_gather(hmat, "col", axis=1, tiled=True),
-        zcolumn,
-        precision=highest,
-        preferred_element_type=jnp.float32,
+        change_tables(hmat), zcolumn, precision=highest, preferred_element_type=jnp.float32
     )
     terms = jnp.dot(
         lax.all_gather(zmat, "col", axis=1, tiled=True).T,

time: 323 us -> 398 us (1.23)
  waiting for transfers between devices: 276 us -> 327 us
  starting transfers between devices: 0.12 us -> 12.9 us
  matrix products: 25.9 us -> 32.3 us
  local copies, waits for them, and re-layouts: 2.11 us -> 6.53 us
    all_to_all x0 -> x1, waiting for transfers between devices: none -> 89.6 us  [reach_pipes(): jax.lax.all_to_all(jnp.stack(tuple((m for _ in range(jax.lax.axis_size(ac...]
    all_gather x1 -> x0, waiting for transfers between devices: 88 us -> none  [local(): lax.all_gather(hmat, 'col', axis=1, tiled=True)]
    all_gather x1, waiting for transfers between devices: 56.9 us -> 137 us  [local(): zcolumn = lax.all_gather(zmat, 'row', axis=0, tiled=True)]
    all_gather x1, waiting for transfers between devices: 76.9 us -> 47.8 us  [local(): lax.all_gather(zmat, 'col', axis=1, tiled=True)]
    all_to_all x0 -> x1, starting transfers between devices: none -> 12.8 us  [reach_pipes(): jax.lax.all_to_all(jnp.stack(tuple((m for _ in range(jax.lax.axis_size(ac...]
    dot_general x1, matrix products: 9.35 us -> 15.8 us  [local(): jnp.dot(change_tables(hmat), zcolumn, precision=highest, preferred_elemen...]
    another operation x0 -> x1, local copies, waits for them, and re-layouts: none -> 4.29 us  [reach_pipes(): jnp.stack(tuple((m for _ in range(jax.lax.axis_size(across)))), axis=0)]
  transfers between devices with their start and end apart: 4 -> 4, of which waited for: 4 -> 4; matrix products, arithmetic and copies ran while one was open for 3% -> 5% of each run, Pallas kernels for 0% -> 0%
where the time goes in v1:
time: 398 us
  waiting for transfers between devices  327 us (82%)
  matrix products  32.3 us (8%)
  between operations  13.2 us (3%)
  starting transfers between devices  12.9 us (3%)
  local copies, waits for them, and re-layouts  6.53 us (2%)
  other arithmetic  5.9 us (1%)
    all_gather x1, waiting for transfers between devices, local(): zcolumn = lax.all_gather(zmat, 'row', axis=0, tiled=True)  137 us
    all_to_all x1, waiting for transfers between devices, reach_pipes(): jax.lax.all_to_all(jnp.stack(tuple((m for _ in range(jax.lax.axis_size(ac...  89.6 us
    reduce_scatter x1, waiting for transfers between devices, local(): result = lax.psum_scatter(terms, 'row', scatter_dimension=0, tiled=True)  52.7 us
    all_gather x1, waiting for transfers between devices, local(): lax.all_gather(zmat, 'col', axis=1, tiled=True)  47.8 us
    dot_general x1, matrix products, local(): jnp.dot(lax.all_gather(zmat, 'col', axis=1, tiled=True).T, hz_tile, preci...  16.5 us
    dot_general x1, matrix products, local(): jnp.dot(change_tables(hmat), zcolumn, precision=highest, preferred_elemen...  15.8 us
    all_to_all x1, starting transfers between devices, reach_pipes(): jax.lax.all_to_all(jnp.stack(tuple((m for _ in range(jax.lax.axis_size(ac...  12.8 us
  transfers between devices with their start and end apart: 4, of which 4 were waited for; matrix products, arithmetic and copies ran while one was open for 5% of the time, Pallas kernels for 0%

profile of v1, /device:TPU:1, one launch (start us, length us, event | category | flops | bytes accessed | tf_op | source)
XLA Modules:
  0.0 398.3 jit_solution(17732666167369030107)
XLA Ops:
  6.5 0.0 all-gather.5.cloned.1.call-start
  6.5 0.7 dynamic_slice.6
  7.3 0.1 convert_bitcast_fusion
  7.3 1.2 dynamic_slice.7
  8.6 0.6 compare_convert_fusion
  9.3 0.7 convert_bitcast_fusion.2
  9.9 0.7 convert_bitcast_fusion.3
  10.6 0.1 broadcast_bitcast_fusion.1
  10.7 2.1 multiply_multiply_fusion
  12.7 0.0 all-gather.5.cloned.1.call-update
  12.7 0.1 copy.7
  12.9 4.3 %stack.2 = f32[32,512,128]{1,2,0:T(8,128)} broadcast(f32[512,128]{0,1:T(8,128)S(1)} %copy.7), dimensions={1,2} | broadcast | bytes 8650752 | tf_op jit(solution)/shard_map/stack | solution.py:13
  17.2 12.8 %all-to-all-start = ((f32[32,512,128]{1,2,0:T(8,128)}), f32[32,512,128]{1,2,0:T(8,128)}, u32[]{:S(2)}, u32[]{:S(2)}) async-start(f32[32,512,128]{1,2,0:T(8,128)} %stack.2), calls=%async_computation | async-start | bytes 16777216 | tf_op jit(solution)/shard_map/all_to_all | solution.py:12
  30.0 0.0 all-gather.3.cloned.1.call-start
  30.0 0.7 all-gather.3.cloned.1.call-update
  30.7 0.0 reduce-scatter.2.cloned.1.call-start
  30.8 136.5 %all-gather.5.cloned.1.call-done = f32[4096,128]{1,0:T(8,128)} async-done(((f32[512,128]{1,0:T(8,128)}), f32[4096,128]{1,0:T(8,128)}) %all-gather.5.cloned.1.call-update) | async-done | bytes 2097168 | tf_op jit(solution)/shard_map/all_gather | solution.py:50
  167.3 89.6 %all-to-all-done = f32[32,512,128]{1,2,0:T(8,128)} async-done(((f32[32,512,128]{1,2,0:T(8,128)}), f32[32,512,128]{1,2,0:T(8,128)}, u32[]{:S(2)}, u32[]{:S(2)}) %all-to-all-start) | async-done | bytes 8388640 | tf_op jit(solution)/shard_map/all_to_all | solution.py:12
  256.9 15.8 %fusion.1 = f32[512,128]{1,0:T(8,128)S(1)} fusion(f32[512,4096]{0,1:T(8,128)} %bitcast.7, f32[4096,128]{1,0:T(8,128)} %all-gather.5.cloned.1.call-done), kind=kOutput, calls=%fused_computation.15 | convolution fusion | flops 3221225472 | bytes 10747904 | tf_op jit(solution)/shard_map/dot_general | solution.py:51
  272.8 0.0 copy-start
  272.8 47.8 %all-gather.3.cloned.1.call-done = f32[512,4096]{1,0:T(8,128)} async-done(((f32[512,128]{1,0:T(8,128)}), f32[512,4096]{1,0:T(8,128)}) %all-gather.3.cloned.1.call-update) | async-done | bytes 8388624 | tf_op jit(solution)/shard_map/all_gather | solution.py:55
  320.6 16.5 %fusion.2 = f32[4096,128]{1,0:T(8,128)} fusion(f32[512,4096]{1,0:T(8,128)} %all-gather.3.cloned.1.call-done, f32[512,128]{1,0:T(8,128)S(1)} %fusion.1), kind=kOutput, calls=%fused_computation.16 | convolution fusion | flops 3221225472 | bytes 10747904 | tf_op jit(solution)/shard_map/dot_general | solution.py:54
  337.1 0.0 reduce-scatter.2.cloned.1.call-update
  337.2 0.0 copy-done
  337.2 0.1 broadcast_bitcast_fusion
  337.2 52.7 %reduce-scatter.2.cloned.1.call-done = f32[512,128]{1,0:T(8,128)} async-done(((f32[4096,128]{1,0:T(8,128)}), f32[512,128]{1,0:T(8,128)}) %reduce-scatter.2.cloned.1.call-update) | async-done | bytes 262160 | tf_op jit(solution)/shard_map/reduce_scatter | solution.py:60
  389.9 1.8 broadcast_multiply_fusion
  (3 shorter events, 0.0 us)
Async XLA Ops:
  6.5 160.8 %all-gather.5.cloned.1.call-start = ((), (), s32[]{:S(2)}) async-start(), calls=%async_computation.3 | async-start | bytes 2359296 | tf_op jit(solution)/shard_map/all_gather | solution.py:50
  17.2 239.7 %all-to-all-start = ((f32[32,512,128]{1,2,0:T(8,128)}), f32[32,512,128]{1,2,0:T(8,128)}, u32[]{:S(2)}, u32[]{:S(2)}) async-start(f32[32,512,128]{1,2,0:T(8,128)} %stack.2), calls=%async_computation | async-start | bytes 16777216 | tf_op jit(solution)/shard_map/all_to_all | solution.py:12
  30.0 290.6 %all-gather.3.cloned.1.call-start = ((), (), s32[]{:S(2)}) async-start(), calls=%async_computation.2 | async-start | bytes 8650752 | tf_op jit(solution)/shard_map/all_gather | solution.py:55
  30.7 359.2 %reduce-scatter.2.cloned.1.call-start = ((), (), s32[]{:S(2)}) async-start(), calls=%async_computation.4 | async-start | bytes 2359296 | tf_op jit(solution)/shard_map/reduce_scatter | solution.py:60
  272.8 64.4 %copy-start = (s32[4,1]{0,1:T(1,128)S(1)}, s32[4,1]{0,1:T(1,128)}, u32[]{:S(2)}) copy-start(s32[4,1]{0,1:T(1,128)} %param.10) | copy-start | bytes 52
Sparse Core Ops, SparseCore 0:
  12.9 154.4 all-gather.4
  169.8 150.7 all-gather.2
  337.3 52.6 reduce-scatter.1
